TPU v7x, 256 devices: a whole 4x4x8 slice. The times are simulated.
256 devices in a mesh: row: 64 (over x, z, core), col: 4 (over y).
Axes of the slice: x: 4, y: 4, z: 8, core: 2. Of those that a mesh axis runs over, the one named last changes fastest.
Arguments:
- pivot_block: float32 [512, 512], P('row', 'col'), as said below
- pivot_tangent: float32 [512, 512], P('row', 'col'), as said below
- panel_block: float32 [65536, 512], P('row', 'col'), may hold values from -1.5 to 1.5
- panel_tangent: float32 [65536, 512], P('row', 'col'), may hold values from -1.5 to 1.5
- strip_block: float32 [65536, 2048], P('row', 'col'), may hold values from -6 to 6
- strip_tangent: float32 [65536, 2048], P('row', 'col'), may hold values from -6 to 6
Outputs:
- pivot_factor: float32 [512, 512], P('row', 'col')
- pivot_factor_tangent: float32 [512, 512], P('row', 'col')
- panel_factor: float32 [65536, 512], P('row', 'col')
- panel_factor_tangent: float32 [65536, 512], P('row', 'col')
- strip_updated: float32 [65536, 2048], P('row', 'col')
- strip_updated_tangent: float32 [65536, 2048], P('row', 'col')
Inputs may be any that keep to these rules, and one draw needn't show every extreme that they name: `pivot_block`: symmetric positive definite; its smallest eigenvalue is at least 0.05. `pivot_tangent`: symmetric.
All inputs are finite; a program needn't handle non-finite values.
Results may differ from a plain program's by a relative error of at most 0.0003.
Values sent between devices are 32-bit elements; how exact they have to be, the bound alone decides.
No kernel may reach another device: no remote copies, remote signals or barrier semaphores. Data moves between devices by JAX's collectives and lax.ppermute only.
A program may use at most 128 MiB of HBM per device.

v0:
```python
import jax
import jax.numpy as jnp
from jax import lax
from jax.sharding import PartitionSpec as P

PIVOT = 512


def outer_product(matrix, others):
    return lax.dot_general(
        matrix,
        others,
        (((1,), (1,)), ((), ())),
        precision=lax.Precision.HIGHEST,
        preferred_element_type=jnp.float32,
    )


def plain_product(matrix, others):
    return jnp.dot(
        matrix, others, precision=lax.Precision.HIGHEST, preferred_element_type=jnp.float32
    )


def body(pivot_block, pivot_tangent, panel_block, panel_tangent, strip_block, strip_tangent):
    row_index = lax.axis_index("row")
    col_index = lax.axis_index("col")
    pivot_rows_local = pivot_block.shape[0]
    pivot_cols_local = pivot_block.shape[1]
    tile_rows = strip_block.shape[1] // lax.axis_size("row")
    stacked = jnp.stack([pivot_block, pivot_tangent])
    halfway = lax.all_gather(stacked, "col", axis=2, tiled=True)
    whole_pivot = lax.all_gather(halfway, "row", axis=1, tiled=True)
    pivot_factor = jnp.linalg.cholesky(whole_pivot[0])
    identity = jnp.eye(PIVOT, dtype=jnp.float32)
    inverse = lax.linalg.triangular_solve(pivot_factor, identity, left_side=True, lower=True)
    mixed = outer_product(plain_product(inverse, whole_pivot[1]), inverse)
    halved = jnp.tril(mixed, -1) + 0.5 * jnp.diag(jnp.diag(mixed))
    pivot_change = plain_product(pivot_factor, halved)
    transposed_inverse = inverse.T
    panel_cols_local = panel_block.shape[1]
    panel_whole = lax.all_gather(jnp.stack([panel_block, panel_tangent]), "col", axis=2, tiled=True)
    panel_factor = plain_product(panel_whole[0], transposed_inverse)
    panel_change = plain_product(
        panel_whole[1] - outer_product(panel_factor, pivot_change), transposed_inverse
    )
    local_rows = panel_block.shape[0]
    own_rows = lax.dynamic_slice_in_dim(
        jnp.stack([panel_factor, panel_change]), col_index * tile_rows, tile_rows, 1
    )
    stacked_panel = jnp.concatenate([panel_factor, panel_change], 0)
    pieces = lax.all_gather(own_rows, "row", axis=1, tiled=True)
    product = outer_product(stacked_panel, pieces[0])
    second_term = outer_product(panel_factor, pieces[1])
    updates = jnp.stack([product[:local_rows], product[local_rows:] + second_term])
    strip_updated = strip_block - updates[0]
    strip_changed = strip_tangent - updates[1]
    corner = (row_index * pivot_rows_local, col_index * pivot_cols_local)
    factor_block = lax.dynamic_slice(pivot_factor, corner, (pivot_rows_local, pivot_cols_local))
    change_block = lax.dynamic_slice(pivot_change, corner, (pivot_rows_local, pivot_cols_local))
    panel_out = lax.dynamic_slice_in_dim(
        panel_factor, col_index * panel_cols_local, panel_cols_local, 1
    )
    panel_change_out = lax.dynamic_slice_in_dim(
        panel_change, col_index * panel_cols_local, panel_cols_local, 1
    )
    return (factor_block, change_block, panel_out, panel_change_out, strip_updated, strip_changed)


def solution(mesh):
    placed = (
        P("row", "col"),
        P("row", "col"),
        P("row", "col"),
        P("row", "col"),
        P("row", "col"),
        P("row", "col"),
    )
    return jax.shard_map(
        body,
        mesh=mesh,
        in_specs=placed,
        out_specs=(
            P("row", "col"),
            P("row", "col"),
            P("row", "col"),
            P("row", "col"),
            P("row", "col"),
            P("row", "col"),
        ),
        check_vma=False,
    )
```

profile of v0, /device:TPU:1, one launch (start us, length us, event | category | flops | bytes accessed | tf_op | source)
XLA Modules:
  0.0 382.7 jit_solution(3954354123918194901)
XLA Ops:
  7.2 0.7 pad_maximum_fusion.2
  7.9 9.4 %all_gather.12 = f32[2,8,512]{2,0,1:T(2,128)} all-gather(f32[2,8,128]{2,0,1:T(2,128)S(1)} %copy.18), channel_id=1, replica_groups=mesh['row'=64,'col'=4] {'col'}, dimensions={2}, use_global_device_ids=true | all-gather | bytes 40960 | tf_op jit(solution)/shard_map/all_gather | solution.py:32
  17.4 2.3 pad_maximum_fusion.1
  19.7 0.8 iota_compare_fusion
  20.5 0.1 fusion.24
  20.7 77.1 %all-gather.4.cloned.1.call-done = f32[2,512,512]{2,0,1:T(2,128)} async-done(((f32[2,8,512]{2,0,1:T(2,128)}), f32[2,512,512]{2,0,1:T(2,128)}) %all-gather.4.cloned.1.call-update) | async-done | bytes 2097168 | tf_op jit(solution)/shard_map/all_gather | solution.py:33
  97.8 5.0 %fusion.59 = (f32[1,512,512]{2,0,1:T(1,128)}, f32[1,512,512]{2,0,1:T(1,128)S(1)}) fusion(f32[2,512,512]{2,0,1:T(2,128)} %all-gather.4.cloned.1.call-done), kind=kLoop, calls=%fused_computation.111 | loop fusion | bytes 4194304 | tf_op jit(solution)/shard_map/slice | solution.py:37
  102.7 1.5 copy.22
  104.2 0.2 fusion.9
  104.5 1.0 copy-done.6
  105.4 11.7 %cholesky.104 = f32[128,128]{1,0:T(8,128)S(1)} custom-call(f32[128,128]{1,0:T(8,128)S(1)} %cholesky.266), custom_call_target="Cholesky" | custom-call | tf_op jit(solution)/shard_map/jit(cholesky)/cholesky | solution.py:34
  117.2 9.8 %custom-call.30 = f32[1,128,128]{1,2,0:T(8,128)S(1)} custom-call(f32[1,128,128]{2,1,0:T(8,128)S(1)} %get-tuple-element.37), custom_call_target="InvertDiagBlocksLowerTriangular" | custom-call | tf_op jit(solution)/shard_map/jit(cholesky)/cholesky | solution.py:34
  127.0 0.1 cholesky.224
  127.1 1.2 constant_dynamic-update-slice_fusion
  128.4 1.3 convolution_subtract_fusion.3
  129.7 11.7 %cholesky.217 = f32[128,128]{1,0:T(8,128)S(1)} custom-call(f32[128,128]{1,0:T(8,128)S(1)} %cholesky.270), custom_call_target="Cholesky" | custom-call | tf_op jit(solution)/shard_map/jit(cholesky)/cholesky | solution.py:34
  141.4 10.0 %custom-call.31 = f32[1,128,128]{1,2,0:T(8,128)S(1)} custom-call(f32[1,128,128]{2,1,0:T(8,128)S(1)} %get-tuple-element.34), custom_call_target="InvertDiagBlocksLowerTriangular" | custom-call | tf_op jit(solution)/shard_map/jit(cholesky)/cholesky | solution.py:34
  151.4 0.3 convolution_dynamic-update-slice_fusion
  151.7 1.3 convolution_subtract_fusion.4
  153.0 11.7 %cholesky.238 = f32[128,128]{1,0:T(8,128)S(1)} custom-call(f32[128,128]{1,0:T(8,128)S(1)} %cholesky.275), custom_call_target="Cholesky" | custom-call | tf_op jit(solution)/shard_map/jit(cholesky)/cholesky | solution.py:34
  164.8 9.8 %custom-call.32 = f32[1,128,128]{1,2,0:T(8,128)S(1)} custom-call(f32[1,128,128]{2,1,0:T(8,128)S(1)} %get-tuple-element.31), custom_call_target="InvertDiagBlocksLowerTriangular" | custom-call | tf_op jit(solution)/shard_map/jit(cholesky)/cholesky | solution.py:34
  174.6 0.2 convolution_dynamic-update-slice_fusion.1
  174.8 1.2 convolution_subtract_fusion.5
  176.0 11.7 %cholesky.255 = f32[128,128]{1,0:T(8,128)S(1)} custom-call(f32[128,128]{1,0:T(8,128)S(1)} %convolution_subtract_fusion.5), custom_call_target="Cholesky" | custom-call | tf_op jit(solution)/shard_map/jit(cholesky)/cholesky | solution.py:34
  187.7 0.6 compare_reduce_fusion.2
  189.7 0.6 compare_reduce_fusion.1
  191.0 0.6 compare_reduce_fusion
  192.3 1.2 fusion.18
  193.5 14.1 %while.1 = (s32[]{:T(128)}, f32[512,512]{1,0:T(8,128)}, s32[4,2]{0,1:T(2,128)S(1)}, f32[4,128,128]{2,1,0:T(8,128)}, s32[]{:T(128)}) while((s32[]{:T(128)}, f32[512,512]{1,0:T(8,128)}, s32[4,2]{0,1:T(2,128)S(1)}, f32[4,128,128]{2,1,0:T(8,128)}, s32[]{:T(128)}) %tuple.33), condition=%wide.while_cond, body=%wide.while_body.sunk | while | flops 2 | bytes 132205 | solution.py:36
  193.5 0.1 constant_dynamic-slice_fusion.4
  193.6 0.6 fusion.72
  194.2 2.9 bitcast_dynamic-update-slice_fusion.2
  197.2 0.5 fusion.72
  197.7 2.9 bitcast_dynamic-update-slice_fusion.2
  200.7 0.5 fusion.72
  201.3 2.9 bitcast_dynamic-update-slice_fusion.2
  204.3 0.5 fusion.72
  204.8 2.9 bitcast_dynamic-update-slice_fusion.2
  207.6 40.5 %custom-call.33 = f32[4,128,128]{1,2,0:T(8,128)S(1)} custom-call(f32[4,128,128]{2,1,0:T(8,128)} %get-tuple-element.13), custom_call_target="InvertDiagBlocksLowerTriangular" | custom-call | tf_op jit(solution)/shard_map/triangular_solve | solution.py:36
  248.2 1.2 fusion.33
  249.4 1.2 convolution_subtract_fusion.1
  250.6 1.4 fusion.45
  252.0 1.4 convolution_subtract_fusion
  253.4 1.3 fusion.43
  254.7 1.7 convolution_subtract_fusion.2
  256.4 1.3 fusion.42
  257.7 1.8 fusion.10
  259.5 1.9 fusion.57
  261.4 4.7 %gather_fusion = f32[512]{0:T(512)S(1)} fusion(f32[512,512]{1,0:T(8,128)S(1)} %fusion.57, s32[512]{0:T(512)S(1)} %bitcast.82), kind=kCustom, calls=%fused_computation | custom fusion | bytes 8192 | tf_op jit(solution)/shard_map/jit(_diag)/jit(diagonal)/cond/branch_0_fun/gather | solution.py:38
  266.1 3.0 fusion.13
  269.1 5.2 %fusion.8 = f32[1024,512]{1,0:T(8,128)S(1)} fusion(f32[2,1024,512]{2,1,0:T(8,128)} %all-gather.6.cloned.1.call-done, f32[128,512]{1,0:T(8,128)S(1)} %fusion.42, f32[128,512]{1,0:T(8,128)S(1)} %fusion.43, f32[128,512]{1,0:T(8,128)S(1)} %fusion.45, f32[128,512]{1,0:T(8,128)S(1)} %fusion.33), kind=kOutput, calls=%fused_computation.16 | convolution fusion | flops 3222011904 | bytes 5242880 | tf_op jit(solution)/shard_map/dot_general | solution.py:20
  274.3 3.5 fusion.60
  277.8 3.7 fusion.6
  281.6 1.3 copy-done
  282.9 0.6 fusion.51
  283.5 1.3 dynamic_slice.15
  284.8 1.3 dynamic_slice.16
  286.1 0.9 constant_dynamic-slice_fusion.2
  287.0 1.9 constant_dynamic-slice_fusion.1
  288.8 69.8 %all-gather.8.cloned.1.call-done = f32[2,512,512]{2,1,0:T(8,128)} async-done(((f32[2,8,512]{2,1,0:T(8,128)}), f32[2,512,512]{2,1,0:T(8,128)}) %all-gather.8.cloned.1.call-update) | async-done | bytes 2097168 | tf_op jit(solution)/shard_map/all_gather | solution.py:52
  358.6 9.3 %fusion = f32[2048,512]{1,0:T(8,128)S(1)} fusion(f32[1024,512]{1,0:T(8,128)} %copy-done, f32[1024,512]{1,0:T(8,128)S(1)} %fusion.8, f32[2,512,512]{2,1,0:T(8,128)} %all-gather.8.cloned.1.call-done), kind=kOutput, calls=%fused_computation.3 | convolution fusion | flops 6443499520 | bytes 9437184 | tf_op jit(solution)/shard_map/dot_general | solution.py:10
  367.9 1.8 slice_subtract_fusion
  369.7 1.1 copy-done.9
  370.8 5.1 %fusion.4 = f32[1024,512]{1,0:T(8,128)} fusion(f32[1024,512]{1,0:T(8,128)S(1)} %copy-done.9, f32[2048,512]{1,0:T(8,128)S(1)} %fusion, f32[1024,512]{1,0:T(8,128)S(1)} %fusion.8, f32[2,512,512]{2,1,0:T(8,128)S(1)} %copy-done.8), kind=kOutput, calls=%fused_computation.10 | convolution fusion | flops 3222274048 | bytes 9437184 | tf_op jit(solution)/shard_map/dot_general | solution.py:10
  (42 shorter events, 0.7 us)
Async XLA Ops:
  7.2 90.6 %all-gather.4.cloned.1.call-start = ((), (), s32[]{:S(2)}) async-start(), calls=%async_computation | async-start | bytes 2129920 | tf_op jit(solution)/shard_map/all_gather | solution.py:33
  17.3 251.8 %all-gather.6.cloned.1.call-start = ((), (), s32[]{:S(2)}) async-start(), calls=%async_computation.1 | async-start | bytes 5242880 | tf_op jit(solution)/shard_map/all_gather | solution.py:42
  19.7 338.9 %all-gather.8.cloned.1.call-start = ((), (), s32[]{:S(2)}) async-start(), calls=%async_computation.2 | async-start | bytes 2129920 | tf_op jit(solution)/shard_map/all_gather | solution.py:52
  20.6 228.7 %copy-start.5 = (f32[512,512]{1,0:T(8,128)}, f32[512,512]{1,0:T(8,128)S(1)}, u32[]{:S(2)}) copy-start(f32[512,512]{1,0:T(8,128)S(1)} %fusion.24) | copy-start | bytes 3145732
  104.5 1.0 copy-start.6
  193.5 72.6 %copy-start.2 = (f32[512,512]{1,0:T(8,128)}, f32[512,512]{1,0:T(8,128)S(1)}, u32[]{:S(2)}) copy-start(f32[512,512]{1,0:T(8,128)S(1)} %get-tuple-element.23) | copy-start | bytes 3145732
  248.2 1.2 copy-start.10
  250.6 7.1 %copy-start.4 = (f32[1,512,512]{2,0,1:T(1,128)S(1)}, f32[1,512,512]{2,0,1:T(1,128)}, u32[]{:S(2)}) copy-start(f32[1,512,512]{2,0,1:T(1,128)} %get-tuple-element.26) | copy-start | bytes 3145732
  269.1 5.2 %copy-start.1 = (f32[512,512]{1,0:T(8,128)S(1)}, f32[512,512]{1,0:T(8,128)}, u32[]{:S(2)}) copy-start(f32[512,512]{1,0:T(8,128)} %fusion.13) | copy-start | bytes 3145732
  274.3 3.5 copy-start.3
  281.6 1.3 copy-start
  358.6 9.3 %copy-start.7 = (f32[1024,512]{1,0:T(8,128)S(1)}, f32[1024,512]{1,0:T(8,128)}, u32[]{:S(2)}) copy-start(f32[1024,512]{1,0:T(8,128)} %param.10) | copy-start | bytes 6291460
  367.9 1.9 copy-start.8
  367.9 3.0 copy-start.9
Sparse Core Ops, SparseCore 0:
  17.4 80.2 all-gather.3
  99.6 51.2 all-gather.5
  283.7 74.8 all-gather.7
where the time goes:
time: 386 us; the launch traced here: 383 us
  waiting for transfers between devices  147 us (38%)
  other arithmetic  127 us (33%)
  matrix products  48.4 us (13%)
  local copies, waits for them, and re-layouts  34.2 us (9%)
  between operations  17 us (4%)
  blocking collectives  9.36 us (2%)
    another operation x14, other arithmetic, body(): pivot_factor = jnp.linalg.cholesky(whole_pivot[0])  78.5 us
    all_gather x1, waiting for transfers between devices, body(): whole_pivot = lax.all_gather(halfway, 'row', axis=1, tiled=True)  77.1 us
    all_gather x1, waiting for transfers between devices, body(): pieces = lax.all_gather(own_rows, 'row', axis=1, tiled=True)  69.8 us
    another operation x3, other arithmetic, body(): lax.linalg.triangular_solve(pivot_factor, identity, left_side=True, lower...  41.7 us
    dot_general x4, matrix products, outer_product(): lax.dot_general(matrix, others, (((1,), (1,)), ((), ())), precision=lax.P...  19.7 us
    another operation x12, local copies, waits for them, and re-layouts  14.1 us
    dot_general x4, matrix products, plain_product(): jnp.dot(matrix, others, precision=lax.Precision.HIGHEST, preferred_elemen...  13.8 us
    another operation x7, matrix products, body(): lax.linalg.triangular_solve(pivot_factor, identity, left_side=True, lower...  9.4 us
  transfers between devices with their start and end apart: 3, of which 2 were waited for; matrix products, arithmetic and copies ran while one was open for 46% of the time, Pallas kernels for 0%

commit v1 on v0

--- a/solution.py
+++ b/solution.py
@@ -49,7 +49,9 @@
         jnp.stack([panel_factor, panel_change]), col_index * tile_rows, tile_rows, 1
     )
     stacked_panel = jnp.concatenate([panel_factor, panel_change], 0)
-    pieces = lax.all_gather(own_rows, "row", axis=1, tiled=True)
+    pieces = jnp.concatenate(
+        lax.all_to_all(jnp.stack([own_rows] * lax.axis_size("row")), "row", 0, 0), axis=1
+    )
     product = outer_product(stacked_panel, pieces[0])
     second_term = outer_product(panel_factor, pieces[1])
     updates = jnp.stack([product[:local_rows], product[local_rows:] + second_term])

time: 386 us -> 371 us (0.961)
  waiting for transfers between devices: 147 us -> 123 us
  starting transfers between devices: 0.12 us -> 6.93 us
    all_gather x1 -> x0, waiting for transfers between devices: 69.8 us -> none  [body(): pieces = lax.all_gather(own_rows, 'row', axis=1, tiled=True)]
    all_to_all x0 -> x1, waiting for transfers between devices: none -> 45.9 us  [body(): lax.all_to_all(jnp.stack([own_rows] * lax.axis_size('row')), 'row', 0, 0)]
    all_to_all x0 -> x1, starting transfers between devices: none -> 6.85 us  [body(): lax.all_to_all(jnp.stack([own_rows] * lax.axis_size('row')), 'row', 0, 0)]
    another operation x12 -> x13, local copies, waits for them, and re-layouts: 14.1 us -> 15.7 us
  transfers between devices with their start and end apart: 3 -> 3, of which waited for: 2 -> 2; matrix products, arithmetic and copies ran while one was open for 46% -> 48% of each run, Pallas kernels for 0% -> 0%
where the time goes in v1:
time: 371 us; the launch traced here: 367 us
  other arithmetic  126 us (34%)
  waiting for transfers between devices  123 us (33%)
  matrix products  49.7 us (13%)
  local copies, waits for them, and re-layouts  34.5 us (9%)
  between operations  17.3 us (5%)
  blocking collectives  9.36 us (3%)
  starting transfers between devices  6.93 us (2%)
    another operation x14, other arithmetic, body(): pivot_factor = jnp.linalg.cholesky(whole_pivot[0])  78.5 us
    all_gather x1, waiting for transfers between devices, body(): whole_pivot = lax.all_gather(halfway, 'row', axis=1, tiled=True)  77.1 us
    all_to_all x1, waiting for transfers between devices, body(): lax.all_to_all(jnp.stack([own_rows] * lax.axis_size('row')), 'row', 0, 0)  45.9 us
    another operation x3, other arithmetic, body(): lax.linalg.triangular_solve(pivot_factor, identity, left_side=True, lower...  41.7 us
    dot_general x4, matrix products, outer_product(): lax.dot_general(matrix, others, (((1,), (1,)), ((), ())), precision=lax.P...  21 us
    another operation x12, local copies, waits for them, and re-layouts  14.1 us
    dot_general x4, matrix products, plain_product(): jnp.dot(matrix, others, precision=lax.Precision.HIGHEST, preferred_elemen...  13.8 us
    another operation x7, matrix products, body(): lax.linalg.triangular_solve(pivot_factor, identity, left_side=True, lower...  9.39 us
  transfers between devices with their start and end apart: 3, of which 2 were waited for; matrix products, arithmetic and copies ran while one was open for 48% of the time, Pallas kernels for 0%

profile of v1, /device:TPU:1, one launch (start us, length us, event | category | flops | bytes accessed | tf_op | source)
XLA Modules:
  0.0 367.1 jit_solution(14787019634981765317)
XLA Ops:
  7.2 0.7 pad_maximum_fusion.2
  7.9 9.4 %all_gather.9 = f32[2,8,512]{2,0,1:T(2,128)} all-gather(f32[2,8,128]{2,0,1:T(2,128)S(1)} %copy.18), channel_id=1, replica_groups=mesh['row'=64,'col'=4] {'col'}, dimensions={2}, use_global_device_ids=true | all-gather | bytes 40960 | tf_op jit(solution)/shard_map/all_gather | solution.py:32
  17.4 2.3 pad_maximum_fusion.1
  19.7 0.8 iota_compare_fusion
  20.5 0.1 fusion.24
  20.6 77.1 %all-gather.3.cloned.1.call-done = f32[2,512,512]{2,0,1:T(2,128)} async-done(((f32[2,8,512]{2,0,1:T(2,128)}), f32[2,512,512]{2,0,1:T(2,128)}) %all-gather.3.cloned.1.call-update) | async-done | bytes 2097168 | tf_op jit(solution)/shard_map/all_gather | solution.py:33
  97.8 5.0 %fusion.59 = (f32[1,512,512]{2,0,1:T(1,128)}, f32[1,512,512]{2,0,1:T(1,128)S(1)}) fusion(f32[2,512,512]{2,0,1:T(2,128)} %all-gather.3.cloned.1.call-done), kind=kLoop, calls=%fused_computation.111 | loop fusion | bytes 4194304 | tf_op jit(solution)/shard_map/slice | solution.py:37
  102.7 1.5 copy.22
  104.2 0.2 fusion.9
  104.5 1.0 copy-done.6
  105.4 11.7 %cholesky.104 = f32[128,128]{1,0:T(8,128)S(1)} custom-call(f32[128,128]{1,0:T(8,128)S(1)} %cholesky.266), custom_call_target="Cholesky" | custom-call | tf_op jit(solution)/shard_map/jit(cholesky)/cholesky | solution.py:34
  117.2 9.8 %custom-call.30 = f32[1,128,128]{1,2,0:T(8,128)S(1)} custom-call(f32[1,128,128]{2,1,0:T(8,128)S(1)} %get-tuple-element.37), custom_call_target="InvertDiagBlocksLowerTriangular" | custom-call | tf_op jit(solution)/shard_map/jit(cholesky)/cholesky | solution.py:34
  127.0 0.1 cholesky.224
  127.1 1.2 constant_dynamic-update-slice_fusion
  128.4 1.3 convolution_subtract_fusion.3
  129.7 11.7 %cholesky.217 = f32[128,128]{1,0:T(8,128)S(1)} custom-call(f32[128,128]{1,0:T(8,128)S(1)} %cholesky.270), custom_call_target="Cholesky" | custom-call | tf_op jit(solution)/shard_map/jit(cholesky)/cholesky | solution.py:34
  141.4 10.0 %custom-call.31 = f32[1,128,128]{1,2,0:T(8,128)S(1)} custom-call(f32[1,128,128]{2,1,0:T(8,128)S(1)} %get-tuple-element.34), custom_call_target="InvertDiagBlocksLowerTriangular" | custom-call | tf_op jit(solution)/shard_map/jit(cholesky)/cholesky | solution.py:34
  151.4 0.3 convolution_dynamic-update-slice_fusion
  151.7 1.3 convolution_subtract_fusion.4
  153.0 11.7 %cholesky.238 = f32[128,128]{1,0:T(8,128)S(1)} custom-call(f32[128,128]{1,0:T(8,128)S(1)} %cholesky.275), custom_call_target="Cholesky" | custom-call | tf_op jit(solution)/shard_map/jit(cholesky)/cholesky | solution.py:34
  164.8 9.8 %custom-call.32 = f32[1,128,128]{1,2,0:T(8,128)S(1)} custom-call(f32[1,128,128]{2,1,0:T(8,128)S(1)} %get-tuple-element.31), custom_call_target="InvertDiagBlocksLowerTriangular" | custom-call | tf_op jit(solution)/shard_map/jit(cholesky)/cholesky | solution.py:34
  174.6 0.2 convolution_dynamic-update-slice_fusion.1
  174.8 1.2 convolution_subtract_fusion.5
  176.0 11.7 %cholesky.255 = f32[128,128]{1,0:T(8,128)S(1)} custom-call(f32[128,128]{1,0:T(8,128)S(1)} %convolution_subtract_fusion.5), custom_call_target="Cholesky" | custom-call | tf_op jit(solution)/shard_map/jit(cholesky)/cholesky | solution.py:34
  187.7 0.6 compare_reduce_fusion.2
  189.7 0.6 compare_reduce_fusion.1
  191.0 0.6 compare_reduce_fusion
  192.3 1.2 fusion.18
  193.5 14.1 %while.1 = (s32[]{:T(128)}, f32[512,512]{1,0:T(8,128)}, s32[4,2]{0,1:T(2,128)S(1)}, f32[4,128,128]{2,1,0:T(8,128)}, s32[]{:T(128)}) while((s32[]{:T(128)}, f32[512,512]{1,0:T(8,128)}, s32[4,2]{0,1:T(2,128)S(1)}, f32[4,128,128]{2,1,0:T(8,128)}, s32[]{:T(128)}) %tuple.33), condition=%wide.while_cond, body=%wide.while_body.sunk | while | flops 2 | bytes 132205 | solution.py:36
  193.5 0.1 constant_dynamic-slice_fusion.4
  193.6 0.6 fusion.72
  194.2 2.9 bitcast_dynamic-update-slice_fusion.2
  197.2 0.5 fusion.72
  197.7 2.9 bitcast_dynamic-update-slice_fusion.2
  200.7 0.5 fusion.72
  201.3 2.9 bitcast_dynamic-update-slice_fusion.2
  204.3 0.5 fusion.72
  204.8 2.9 bitcast_dynamic-update-slice_fusion.2
  207.6 40.5 %custom-call.33 = f32[4,128,128]{1,2,0:T(8,128)S(1)} custom-call(f32[4,128,128]{2,1,0:T(8,128)} %get-tuple-element.13), custom_call_target="InvertDiagBlocksLowerTriangular" | custom-call | tf_op jit(solution)/shard_map/triangular_solve | solution.py:36
  248.2 1.2 fusion.33
  249.4 1.2 convolution_subtract_fusion.1
  250.6 1.3 fusion.45
  252.0 1.4 convolution_subtract_fusion
  253.4 1.3 fusion.43
  254.7 1.7 convolution_subtract_fusion.2
  256.4 1.3 fusion.42
  257.7 1.8 fusion.10
  259.5 1.9 fusion.57
  261.4 4.7 %gather_fusion = f32[512]{0:T(512)S(1)} fusion(f32[512,512]{1,0:T(8,128)S(1)} %fusion.57, s32[512]{0:T(512)S(1)} %bitcast.83), kind=kCustom, calls=%fused_computation | custom fusion | bytes 8192 | tf_op jit(solution)/shard_map/jit(_diag)/jit(diagonal)/cond/branch_0_fun/gather | solution.py:38
  266.1 3.1 fusion.13
  269.2 5.2 %fusion.8 = f32[1024,512]{1,0:T(8,128)S(1)} fusion(f32[2,1024,512]{2,1,0:T(8,128)} %all-gather.5.cloned.1.call-done, f32[128,512]{1,0:T(8,128)S(1)} %fusion.42, f32[128,512]{1,0:T(8,128)S(1)} %fusion.43, f32[128,512]{1,0:T(8,128)S(1)} %fusion.45, f32[128,512]{1,0:T(8,128)S(1)} %fusion.33), kind=kOutput, calls=%fused_computation.16 | convolution fusion | flops 3222011904 | bytes 5242880 | tf_op jit(solution)/shard_map/dot_general | solution.py:20
  274.4 3.5 fusion.60
  277.9 3.7 %fusion.6 = f32[1024,512]{1,0:T(8,128)S(1)} fusion(f32[1024,512]{1,0:T(8,128)S(1)} %fusion.60, f32[2,1024,512]{2,1,0:T(8,128)S(1)} %copy-done.3, f32[128,512]{1,0:T(8,128)S(1)} %fusion.42, f32[128,512]{1,0:T(8,128)S(1)} %fusion.43, f32[128,512]{1,0:T(8,128)S(1)} %fusion.45, f32[128,512]{1,0:T(8,128)S(1)} %fusion.33), kind=kOutput, calls=%fused_computation.14 | convolution fusion | flops 3222536192 | bytes 7340032 | tf_op jit(solution)/shard_map/dot_general | solution.py:20
  281.6 1.3 copy-done
  282.9 1.6 stack.29
  284.5 6.8 %all-to-all-start = ((f32[64,2,8,512]{3,2,1,0:T(8,128)}), f32[64,2,8,512]{3,2,1,0:T(8,128)}, u32[]{:S(2)}, u32[]{:S(2)}) async-start(f32[64,2,8,512]{3,2,1,0:T(8,128)} %stack.29), calls=%async_computation | async-start | bytes 4194304 | tf_op jit(solution)/shard_map/all_to_all | solution.py:53
  291.4 1.3 dynamic_slice.15
  292.7 1.3 dynamic_slice.16
  293.9 0.9 constant_dynamic-slice_fusion.2
  294.8 1.9 constant_dynamic-slice_fusion.1
  296.6 45.9 %all-to-all-done = f32[64,2,8,512]{3,2,1,0:T(8,128)} async-done(((f32[64,2,8,512]{3,2,1,0:T(8,128)}), f32[64,2,8,512]{3,2,1,0:T(8,128)}, u32[]{:S(2)}, u32[]{:S(2)}) %all-to-all-start) | async-done | bytes 2097184 | tf_op jit(solution)/shard_map/all_to_all | solution.py:53
  342.5 9.3 %fusion = f32[2048,512]{1,0:T(8,128)S(1)} fusion(f32[1024,512]{1,0:T(8,128)} %copy-done, f32[1024,512]{1,0:T(8,128)S(1)} %fusion.8, f32[2,64,8,512]{3,2,0,1:T(8,128)} %bitcast.21), kind=kOutput, calls=%fused_computation.3 | convolution fusion | flops 6443499520 | bytes 9437184 | tf_op jit(solution)/shard_map/dot_general | solution.py:10
  351.8 6.4 %fusion.4 = f32[1024,512]{1,0:T(8,128)} fusion(f32[1024,512]{1,0:T(8,128)S(1)} %copy-done.8, f32[2048,512]{1,0:T(8,128)S(1)} %fusion, f32[1024,512]{1,0:T(8,128)S(1)} %fusion.8, f32[2,64,8,512]{3,2,0,1:T(8,128)} %bitcast.21), kind=kOutput, calls=%fused_computation.10 | convolution fusion | flops 3222274048 | bytes 9437184 | tf_op jit(solution)/shard_map/dot_general | solution.py:10
  358.2 1.8 slice_subtract_fusion
  (40 shorter events, 0.6 us)
Async XLA Ops:
  7.2 90.6 %all-gather.3.cloned.1.call-start = ((), (), s32[]{:S(2)}) async-start(), calls=%async_computation.1 | async-start | bytes 2129920 | tf_op jit(solution)/shard_map/all_gather | solution.py:33
  17.3 251.9 %all-gather.5.cloned.1.call-start = ((), (), s32[]{:S(2)}) async-start(), calls=%async_computation.2 | async-start | bytes 5242880 | tf_op jit(solution)/shard_map/all_gather | solution.py:42
  20.6 228.8 %copy-start.5 = (f32[512,512]{1,0:T(8,128)}, f32[512,512]{1,0:T(8,128)S(1)}, u32[]{:S(2)}) copy-start(f32[512,512]{1,0:T(8,128)S(1)} %fusion.24) | copy-start | bytes 3145732
  104.5 1.0 copy-start.6
  193.5 72.6 %copy-start.2 = (f32[512,512]{1,0:T(8,128)}, f32[512,512]{1,0:T(8,128)S(1)}, u32[]{:S(2)}) copy-start(f32[512,512]{1,0:T(8,128)S(1)} %get-tuple-element.23) | copy-start | bytes 3145732
  248.1 1.2 copy-start.9
  250.6 7.1 %copy-start.4 = (f32[1,512,512]{2,0,1:T(1,128)S(1)}, f32[1,512,512]{2,0,1:T(1,128)}, u32[]{:S(2)}) copy-start(f32[1,512,512]{2,0,1:T(1,128)} %get-tuple-element.26) | copy-start | bytes 3145732
  269.2 5.2 %copy-start.1 = (f32[512,512]{1,0:T(8,128)S(1)}, f32[512,512]{1,0:T(8,128)}, u32[]{:S(2)}) copy-start(f32[512,512]{1,0:T(8,128)} %fusion.13) | copy-start | bytes 3145732
  274.3 3.5 copy-start.3
  281.6 1.3 copy-start
  284.5 58.0 %all-to-all-start = ((f32[64,2,8,512]{3,2,1,0:T(8,128)}), f32[64,2,8,512]{3,2,1,0:T(8,128)}, u32[]{:S(2)}, u32[]{:S(2)}) async-start(f32[64,2,8,512]{3,2,1,0:T(8,128)} %stack.29), calls=%async_computation | async-start | bytes 4194304 | tf_op jit(solution)/shard_map/all_to_all | solution.py:53
  342.5 9.3 %copy-start.8 = (f32[1024,512]{1,0:T(8,128)S(1)}, f32[1024,512]{1,0:T(8,128)}, u32[]{:S(2)}) copy-start(f32[1024,512]{1,0:T(8,128)} %param.11) | copy-start | bytes 6291460
  351.8 6.4 %copy-start.7 = (f32[1024,512]{1,0:T(8,128)S(1)}, f32[1024,512]{1,0:T(8,128)}, u32[]{:S(2)}) copy-start(f32[1024,512]{1,0:T(8,128)} %param.10) | copy-start | bytes 6291460
Sparse Core Ops, SparseCore 0:
  17.4 80.2 all-gather.2
  99.6 51.2 all-gather.4
